TPU v7x, 32 devices: a whole 2x2x4 slice. The times are simulated.
32 devices in a mesh: grp: 4 (over y, x), col: 8 (over z, core).
Axes of the slice: x: 2, y: 2, z: 4, core: 2. Of those that a mesh axis runs over, the one named last changes fastest.
Arguments:
- right_side: float32 [2048, 2048], P('grp', 'col'), may hold values from -6 to 6
- solved_factor: float32 [2048, 6144], P('grp', 'col'), may hold values from -0.078125 to 0.078125
- solved_users: float32 [6144, 2048], P('col'), may hold values from -6 to 6
- diag_inverse: float32 [2048, 512], P('grp'), may hold values from -0.25 to 0.25
- coupling: float32 [2048, 1536], P('grp'), may hold values from -0.25 to 0.25
Outputs:
- solution: float32 [2048, 2048], P('grp', 'col')
All inputs are finite; a program needn't handle non-finite values.
Results may differ from a plain program's by a relative error of at most 0.0001.
Values sent between devices are 32-bit elements; how exact they have to be, the bound alone decides.
A program may use at most 64 MiB of HBM per device.

v0:
```python
import jax
import jax.numpy as jnp
from jax import lax
from jax.sharding import PartitionSpec as P

highest = lax.Precision.HIGHEST


def broadcast(block, axis, source):
    block = jnp.where(lax.axis_index(axis) == source, block, jnp.zeros_like(block))
    return lax.psum(block, axis)


def apply_plain(matrix, vector):
    return jnp.dot(matrix, vector, precision=highest, preferred_element_type=jnp.float32)


def run_chain(residue, diag_inverse, coupling, apply_left):
    groups = lax.axis_size("grp")
    position = lax.axis_index("grp")
    block_rows = diag_inverse.shape[0]
    result = jnp.zeros_like(residue)
    for section_index in range(groups):
        candidate = apply_left(diag_inverse, residue)
        result = jnp.where(position == section_index, candidate, result)
        if section_index + 1 < groups:
            solved = broadcast(candidate, "grp", section_index)
            coupling_block = coupling[
                :, section_index * block_rows : (section_index + 1) * block_rows
            ]
            residue = jnp.where(
                position > section_index, residue - apply_left(coupling_block, solved), residue
            )
    return result


def on_device(right_side, solved_factor, solved_users, diag_inverse, coupling):
    partials = jnp.dot(
        solved_factor, solved_users, precision=highest, preferred_element_type=jnp.float32
    )
    shares = lax.psum_scatter(partials, "col", scatter_dimension=1, tiled=True)
    residue = right_side - shares
    return run_chain(residue, diag_inverse, coupling, apply_plain)


def solution(mesh):
    placed = (P("grp", "col"), P("grp", "col"), P("col", None), P("grp", None), P("grp", None))
    return jax.shard_map(
        on_device, mesh=mesh, in_specs=placed, out_specs=P("grp", "col"), check_vma=False
    )
```

profile of v0, /device:TPU:7, one launch (start us, length us, event | category | flops | bytes accessed | tf_op | source)
XLA Modules:
  0.0 236.7 jit_solution(10493149268610396143)
XLA Ops:
  6.5 1.4 copy-done
  7.9 13.7 %fusion.11 = f32[512,2048]{1,0:T(8,128)} fusion(f32[512,768]{1,0:T(8,128)S(1)} %copy-done, f32[768,2048]{1,0:T(8,128)} %param.7), kind=kOutput, calls=%fused_computation.20 | convolution fusion | flops 9663676416 | bytes 12058624 | tf_op jit(solution)/shard_map/dot_general | solution.py:38
  21.7 0.0 reduce-scatter.2.cloned.1.call-update
  21.7 0.0 all-reduce.4.cloned.1.call-start
  21.8 49.3 %reduce-scatter.2.cloned.1.call-done = f32[512,256]{1,0:T(8,128)} async-done(((f32[512,2048]{1,0:T(8,128)}), f32[512,256]{1,0:T(8,128)}) %reduce-scatter.2.cloned.1.call-update) | async-done | bytes 524304 | tf_op jit(solution)/shard_map/reduce_scatter | solution.py:41
  71.1 1.3 sub.12
  72.4 2.7 %fusion.7 = f32[512,256]{0,1:T(8,128)} fusion(f32[512,256]{1,0:T(8,128)S(1)} %sub.12, f32[512,512]{1,0:T(8,128)S(1)} %copy-done.1, pred[]{:T(512)S(6)} %eq.16), kind=kOutput, calls=%fused_computation.14 | convolution fusion | flops 805437440 | bytes 2097153 | tf_op jit(solution)/shard_map/dot_general | solution.py:15
  75.0 0.0 all-reduce.4.cloned.1.call-update
  75.1 0.0 all-reduce.6.cloned.1.call-start
  75.1 44.4 %all-reduce.4.cloned.1.call-done = f32[512,256]{0,1:T(8,128)} async-done(((f32[512,256]{0,1:T(8,128)}), f32[512,256]{0,1:T(8,128)}) %all-reduce.4.cloned.1.call-update) | async-done | bytes 524304 | tf_op jit(solution)/shard_map/psum | solution.py:11
  119.5 2.4 %fusion.6 = f32[512,256]{1,0:T(8,128)S(1)} fusion(f32[512,256]{1,0:T(8,128)S(1)} %sub.12, f32[512,256]{0,1:T(8,128)} %all-reduce.4.cloned.1.call-done, f32[512,1536]{1,0:T(8,128)} %param.9, pred[]{:T(512)S(6)} %gt.11), kind=kOutput, calls=%fused_computation.12 | convolution fusion | flops 805568512 | bytes 2621441 | tf_op jit(solution)/shard_map/dot_general | solution.py:15
  121.9 0.8 copy-done.3
  122.7 2.8 %broadcast_select_fusion.1 = (f32[512,256]{0,1:T(8,128)}, f32[512,256]{0,1:T(8,128)}) fusion(pred[]{:T(512)S(6)} %eq.17, f32[512,256]{1,0:T(8,128)S(1)} %fusion.6, f32[512,512]{1,0:T(8,128)S(1)} %copy-done.1), kind=kOutput, calls=%fused_computation.19 | convolution fusion | flops 805437440 | bytes 2621441 | tf_op jit(solution)/shard_map/dot_general | solution.py:15
  125.6 0.0 all-reduce.6.cloned.1.call-update
  125.6 0.2 all-reduce.8.cloned.1.call-start
  125.8 45.3 %all-reduce.6.cloned.1.call-done = f32[512,256]{0,1:T(8,128)} async-done(((f32[512,256]{0,1:T(8,128)}), f32[512,256]{0,1:T(8,128)}) %all-reduce.6.cloned.1.call-update) | async-done | bytes 524304 | tf_op jit(solution)/shard_map/psum | solution.py:11
  171.1 2.5 %fusion.4 = f32[512,256]{1,0:T(8,128)S(1)} fusion(f32[512,256]{1,0:T(8,128)} %copy-done.3, f32[512,256]{0,1:T(8,128)} %all-reduce.6.cloned.1.call-done, f32[512,1536]{1,0:T(8,128)} %param.9, pred[]{:T(512)S(6)} %gt.10), kind=kOutput, calls=%fused_computation.8 | convolution fusion | flops 805568512 | bytes 2621441 | tf_op jit(solution)/shard_map/dot_general | solution.py:15
  173.7 0.8 copy-done.4
  174.5 2.8 %broadcast_select_fusion = (f32[512,256]{0,1:T(8,128)}, f32[512,256]{0,1:T(8,128)}) fusion(pred[]{:T(512)S(6)} %eq.18, f32[512,256]{1,0:T(8,128)S(1)} %fusion.4, f32[512,512]{1,0:T(8,128)S(1)} %copy-done.1), kind=kOutput, calls=%fused_computation.18 | convolution fusion | flops 805437440 | bytes 2621441 | tf_op jit(solution)/shard_map/dot_general | solution.py:15
  177.3 0.0 all-reduce.8.cloned.1.call-update
  177.3 45.5 %all-reduce.8.cloned.1.call-done = f32[512,256]{0,1:T(8,128)} async-done(((f32[512,256]{0,1:T(8,128)}), f32[512,256]{0,1:T(8,128)}) %all-reduce.8.cloned.1.call-update) | async-done | bytes 524304 | tf_op jit(solution)/shard_map/psum | solution.py:11
  222.9 2.5 %fusion.2 = f32[512,256]{1,0:T(8,128)S(1)} fusion(f32[512,256]{1,0:T(8,128)} %copy-done.4, f32[512,256]{0,1:T(8,128)} %all-reduce.8.cloned.1.call-done, f32[512,1536]{1,0:T(8,128)} %param.9, pred[]{:T(512)S(6)} %gt.9), kind=kOutput, calls=%fused_computation.4 | convolution fusion | flops 805568512 | bytes 2621441 | tf_op jit(solution)/shard_map/dot_general | solution.py:15
  225.4 2.7 %fusion = f32[512,256]{0,1:T(8,128)} fusion(f32[512,256]{1,0:T(8,128)S(1)} %fusion.2, f32[512,512]{1,0:T(8,128)S(1)} %copy-done.1, f32[512,256]{0,1:T(8,128)} %get-tuple-element.8, f32[512,256]{0,1:T(8,128)} %get-tuple-element.6, f32[512,256]{0,1:T(8,128)S(1)} %copy-done.2, pred[]{:T(512)S(6)} %eq.18, pred[]{:T(512)S(6)} %eq.17, pred[]{:T(512)S(6)} %eq.15), kind=kOutput, calls=%fused_computation.1 | convolution fusion | flops 805699584 | bytes 3670019 | tf_op jit(solution)/shard_map/dot_general | solution.py:15
  228.1 2.0 copy.8
  (8 shorter events, 0.0 us)
Async XLA Ops:
  6.5 1.4 copy-start
  6.5 64.6 %reduce-scatter.2.cloned.1.call-start = ((), (), s32[]{:S(2)}) async-start(), calls=%async_computation.1 | async-start | bytes 4718592 | tf_op jit(solution)/shard_map/reduce_scatter | solution.py:41
  21.7 50.7 %copy-start.1 = (f32[512,512]{1,0:T(8,128)S(1)}, f32[512,512]{1,0:T(8,128)}, u32[]{:S(2)}) copy-start(f32[512,512]{1,0:T(8,128)} %param.8) | copy-start | bytes 3145732
  21.7 97.8 %all-reduce.4.cloned.1.call-start = ((), (), s32[]{:S(2)}) async-start(), calls=%async_computation.2 | async-start | bytes 1048576 | tf_op jit(solution)/shard_map/psum | solution.py:11
  75.1 96.0 %all-reduce.6.cloned.1.call-start = ((), (), s32[]{:S(2)}) async-start(), calls=%async_computation.3 | async-start | bytes 1048576 | tf_op jit(solution)/shard_map/psum | solution.py:11
  121.9 0.8 copy-start.3
  125.6 97.3 %all-reduce.8.cloned.1.call-start = ((), (), s32[]{:S(2)}) async-start(), calls=%async_computation.4 | async-start | bytes 1048576 | tf_op jit(solution)/shard_map/psum | solution.py:11
  173.6 0.8 copy-start.4
  174.5 51.0 %copy-start.2 = (f32[512,256]{0,1:T(8,128)S(1)}, f32[512,256]{0,1:T(8,128)}, u32[]{:S(2)}) copy-start(f32[512,256]{0,1:T(8,128)} %fusion.7) | copy-start | bytes 1572868
Sparse Core Ops, SparseCore 0:
  21.8 49.2 reduce-scatter.1
  75.2 44.2 all-reduce.3
  125.7 45.3 all-reduce.5
  177.5 45.3 all-reduce.7
where the time goes:
time: 240 us; the launch traced here: 237 us
  waiting for transfers between devices  185 us (77%)
  matrix products  32.3 us (13%)
  between operations  13.2 us (6%)
  local copies, waits for them, and re-layouts  5.04 us (2%)
    psum x3, waiting for transfers between devices, broadcast(): return lax.psum(block, axis)  135 us
    reduce_scatter x1, waiting for transfers between devices, on_device(): shares = lax.psum_scatter(partials, 'col', scatter_dimension=1, tiled=True)  49.3 us
    dot_general x7, matrix products, apply_plain(): jnp.dot(matrix, vector, precision=highest, preferred_element_type=jnp.flo...  18.6 us
    dot_general x1, matrix products, on_device(): jnp.dot(solved_factor, solved_users, precision=highest, preferred_element...  13.7 us
  transfers between devices with their start and end apart: 4, of which 4 were waited for; matrix products, arithmetic and copies ran while one was open for 0% of the time, Pallas kernels for 0%

commit v1 on v0

--- a/solution.py
+++ b/solution.py
@@ -1,9 +1,15 @@
+import functools
+
 import jax
 import jax.numpy as jnp
 from jax import lax
+from jax.experimental import pallas as pl
+from jax.experimental.pallas import tpu as pltpu
 from jax.sharding import PartitionSpec as P
 
 highest = lax.Precision.HIGHEST
+MESH = pl.DeviceIdType.MESH
+LANES = 128
 
 
 def broadcast(block, axis, source):
@@ -34,7 +40,7 @@
     return result
 
 
-def on_device(right_side, solved_factor, solved_users, diag_inverse, coupling):
+def by_collectives(right_side, solved_factor, solved_users, diag_inverse, coupling):
     partials = jnp.dot(
         solved_factor, solved_users, precision=highest, preferred_element_type=jnp.float32
     )
@@ -43,6 +49,316 @@
     return run_chain(residue, diag_inverse, coupling, apply_plain)
 
 
+def halves(x):
+    high = x.astype(jnp.bfloat16)
+    return high, (x - high.astype(jnp.float32)).astype(jnp.bfloat16)
+
+
+def left_form(x):
+    high, low = halves(x)
+    return jnp.concatenate([high, high, low], axis=1)
+
+
+def right_form(x):
+    high, low = halves(x)
+    return jnp.concatenate([high, low, high], axis=0)
+
+
+def dot(a, b):
+    return jnp.dot(a, b, preferred_element_type=jnp.float32)
+
+
+def kernel(
+    groups, chips, pieces,
+    rhs_hbm, factor_hbm, users_hbm, diag_hbm, coupling_hbm,
+    out_ref,
+    rhs, factor, users, diag, coupling,
+    factor3, diag3, effect3,
+    own, give, take, from_low, from_high, total, spare, solved, arrived,
+    load_sem, users_sem, give_sem, take_sem, hop_sem, low_sem, high_sem,
+    spare_sem, total_sem, solved_sem, arrived_sem,
+):
+    g = lax.axis_index("grp")
+    c = lax.axis_index("col")
+    z = c // 2
+    e = c % 2
+    rows = rhs.shape[0]
+    half = rows // 2
+    width = rhs.shape[1]
+    partner = (g, z * 2 + (1 - e))
+    above = (g, c + 2)
+    below = (g, c - 2)
+
+    def block_of(b):
+        j = b % chips
+        return (b // chips) * chips + jnp.where(2 * z < chips, chips - 1 - j, j)
+
+    loads = []
+    for part in range(2):
+        source = pl.multiple_of((e if part == 0 else 1 - e) * half, half)
+        loads.append(pltpu.make_async_copy(
+            factor_hbm.at[pl.ds(source, half)], factor.at[pl.ds(part * half, half)],
+            load_sem.at[part]))
+    later = [
+        pltpu.make_async_copy(diag_hbm, diag, load_sem.at[2]),
+        pltpu.make_async_copy(coupling_hbm, coupling, load_sem.at[3]),
+        pltpu.make_async_copy(rhs_hbm, rhs, load_sem.at[4]),
+    ]
+
+    def users_load(b):
+        i = block_of(b)
+        column = pl.multiple_of(((i % chips) * 2 + i // chips) * width, width)
+        return pltpu.make_async_copy(
+            users_hbm.at[:, pl.ds(column, width)], users.at[b], users_sem.at[b])
+
+    for copy in loads:
+        copy.start()
+
+    @pl.loop(0, 2 * chips)
+    def _(b):
+        users_load(b).start()
+
+    for copy in later:
+        copy.start()
+
+    barrier = pltpu.get_barrier_semaphore()
+    pl.semaphore_signal(barrier, inc=1, device_id=partner, device_id_type=MESH)
+    for step in range(1, groups):
+        pl.semaphore_signal(
+            barrier, inc=1, device_id=((g + step) % groups, c), device_id_type=MESH)
+
+    @pl.when(z > 0)
+    def _():
+        pl.semaphore_signal(barrier, inc=1, device_id=below, device_id_type=MESH)
+
+    @pl.when(z < chips - 1)
+    def _():
+        pl.semaphore_signal(barrier, inc=1, device_id=above, device_id_type=MESH)
+
+    pl.semaphore_wait(
+        barrier, groups + jnp.where(z > 0, 1, 0) + jnp.where(z < chips - 1, 1, 0))
+
+    for copy in loads:
+        copy.wait()
+    factor3[...] = left_form(factor[...])
+
+    def give_copy(i):
+        return pltpu.make_async_remote_copy(
+            src_ref=give.at[i], dst_ref=take.at[i], send_sem=give_sem.at[i],
+            recv_sem=take_sem.at[i], device_id=partner, device_id_type=MESH)
+
+    def up(i, q):
+        return pltpu.make_async_remote_copy(
+            src_ref=own.at[i, q], dst_ref=from_low.at[i, q], send_sem=hop_sem.at[i, q],
+            recv_sem=low_sem.at[i, q], device_id=above, device_id_type=MESH)
+
+    def down(i, q):
+        return pltpu.make_async_remote_copy(
+            src_ref=own.at[i, q], dst_ref=from_high.at[i, q], send_sem=hop_sem.at[i, q],
+            recv_sem=high_sem.at[i, q], device_id=below, device_id_type=MESH)
+
+    def send_first(i, q):
+        d = i % chips
+
+        @pl.when(jnp.logical_and(z == 0, d > 0))
+        def _():
+            up(i, q).start()
+
+        if chips > 1:
+            @pl.when(jnp.logical_and(z == chips - 1, d < chips - 1))
+            def _():
+                down(i, q).start()
+
+    def merge(b):
+        i = block_of(b)
+        give_copy(i).wait()
+        own[i] = own[i] + take[i]
+        send_first(i, 0)
+
+    @pl.loop(0, 2 * chips)
+    def _(b):
+        users_load(b).wait()
+        i = block_of(b)
+        product = dot(factor3[...], right_form(users[b]))
+        for q in range(pieces):
+            columns = slice(q * LANES, (q + 1) * LANES)
+            own[i, q] = product[:half, columns]
+            give[i, q] = product[half:, columns]
+        give_copy(i).start()
+
+        @pl.when(b > 0)
+        def _():
+            merge(b - 1)
+
+    merge(2 * chips - 1)
+    for q in range(1, pieces):
+        @pl.loop(0, 2 * chips)
+        def _(b):
+            send_first(block_of(b), q)
+
+    for copy in later:
+        copy.wait()
+    diag3[...] = left_form(diag[...])
+    for h in range(groups - 1):
+        @pl.loop(0, rows // (2 * LANES))
+        def _(n):
+            columns = pl.multiple_of(n * 2 * LANES, 2 * LANES)
+            product = dot(
+                diag3[...], right_form(coupling[:, pl.ds(h * rows + columns, 2 * LANES)]))
+            high, low = halves(product)
+            effect3[h, :, pl.ds(columns, 2 * LANES)] = high
+            effect3[h, :, pl.ds(rows + columns, 2 * LANES)] = high
+            effect3[h, :, pl.ds(2 * rows + columns, 2 * LANES)] = low
+
+    def total_copy(side, q):
+        start = pl.multiple_of(e * half, half)
+        return pltpu.make_async_remote_copy(
+            src_ref=spare.at[q], dst_ref=total.at[q, pl.ds(start, half)],
+            send_sem=spare_sem.at[q], recv_sem=total_sem.at[q],
+            device_id=partner, device_id_type=MESH)
+
+    def reduce_piece(p):
+        q = p // 2
+        side = p % 2
+        for s in range(chips - 1):
+            right = side * chips + chips - 1 - s
+            left = side * chips + s
+
+            @pl.when(jnp.logical_and(z > 0, chips - 1 - s > z))
+            def _():
+                up(right, q).wait_recv()
+                own[right, q] = own[right, q] + from_low[right, q]
+                up(right, q).start()
+
+            @pl.when(jnp.logical_and(z < chips - 1, s < z))
+            def _():
+                down(left, q).wait_recv()
+                own[left, q] = own[left, q] + from_high[left, q]
+                down(left, q).start()
+
+        mine = side * chips + z
+
+        @pl.when(z > 0)
+        def _():
+            up(mine, q).wait_recv()
+            own[mine, q] = own[mine, q] + from_low[mine, q]
+
+        @pl.when(z < chips - 1)
+        def _():
+            down(mine, q).wait_recv()
+            own[mine, q] = own[mine, q] + from_high[mine, q]
+
+        @pl.when(side == e)
+        def _():
+            total[q, pl.ds(pl.multiple_of(e * half, half), half)] = own[mine, q]
+
+        @pl.when(side != e)
+        def _():
+            spare[q] = own[mine, q]
+            total_copy(side, q).start()
+
+    def solved_copy(source, target, q):
+        return pltpu.make_async_remote_copy(
+            src_ref=solved.at[q], dst_ref=arrived.at[source, q],
+            send_sem=solved_sem.at[target, q], recv_sem=arrived_sem.at[source, q],
+            device_id=(target, c), device_id_type=MESH)
+
+    def solve_piece(q):
+        columns = pl.ds(pl.multiple_of(q * LANES, LANES), LANES)
+        total_copy(e, q).wait_recv()
+        solved[q] = dot(diag3[...], right_form(rhs[:, columns] - total[q]))
+        for h in range(groups - 1):
+            @pl.when(h < g)
+            def _():
+                solved_copy(h, 0, q).wait_recv()
+                solved[q] = solved[q] - dot(effect3[h], right_form(arrived[h, q]))
+        for target in range(1, groups):
+            @pl.when(target > g)
+            def _():
+                solved_copy(g, target, q).start()
+        out_ref[:, columns] = solved[q]
+
+    count = 2 * pieces
+
+    @pl.loop(0, count + groups - 1)
+    def _(t):
+        @pl.when(t < count)
+        def _():
+            reduce_piece(t)
+
+        p = t - g
+
+        @pl.when(jnp.logical_and(jnp.logical_and(p >= 0, p < count), (p + 2 * groups) % 2 == e))
+        def _():
+            solve_piece(p // 2)
+
+    @pl.loop(0, 2 * chips)
+    def _(i):
+        @pl.when(i % chips != z)
+        def _():
+            for q in range(pieces):
+                pltpu.make_async_remote_copy(
+                    src_ref=own.at[i, q], dst_ref=from_low.at[i, q], send_sem=hop_sem.at[i, q],
+                    recv_sem=low_sem.at[i, q], device_id=partner, device_id_type=MESH
+                ).wait_send()
+
+    for q in range(pieces):
+        total_copy(0, q).wait_send()
+        for target in range(1, groups):
+            @pl.when(target > g)
+            def _():
+                solved_copy(g, target, q).wait_send()
+
+
+def by_kernel(right_side, solved_factor, solved_users, diag_inverse, coupling):
+    groups = lax.axis_size("grp")
+    chips = lax.axis_size("col") // 2
+    rows, width = right_side.shape
+    depth = solved_factor.shape[1]
+    half = rows // 2
+    pieces = width // LANES
+    f32, bf16 = jnp.float32, jnp.bfloat16
+    unit = (half, LANES)
+    blocks = 2 * chips
+    dma = pltpu.SemaphoreType.DMA
+    scratch = [
+        pltpu.VMEM((rows, width), f32),
+        pltpu.VMEM((rows, depth), f32),
+        pltpu.VMEM((blocks, depth, width), f32),
+        pltpu.VMEM((rows, rows), f32),
+        pltpu.VMEM(coupling.shape, f32),
+        pltpu.VMEM((rows, 3 * depth), bf16),
+        pltpu.VMEM((rows, 3 * rows), bf16),
+        pltpu.VMEM((groups - 1, rows, 3 * rows), bf16),
+        pltpu.VMEM((blocks, pieces) + unit, f32),
+        pltpu.VMEM((blocks, pieces) + unit, f32),
+        pltpu.VMEM((blocks, pieces) + unit, f32),
+        pltpu.VMEM((blocks, pieces) + unit, f32),
+        pltpu.VMEM((blocks, pieces) + unit, f32),
+        pltpu.VMEM((pieces, rows, LANES), f32),
+        pltpu.VMEM((pieces,) + unit, f32),
+        pltpu.VMEM((pieces, rows, LANES), f32),
+        pltpu.VMEM((groups - 1, pieces, rows, LANES), f32),
+        dma((5,)), dma((blocks,)), dma((blocks,)), dma((blocks,)),
+        dma((blocks, pieces)), dma((blocks, pieces)), dma((blocks, pieces)),
+        dma((pieces,)), dma((pieces,)), dma((groups, pieces)), dma((groups, pieces)),
+    ]
+    return pl.pallas_call(
+        functools.partial(kernel, groups, chips, pieces),
+        out_shape=jax.ShapeDtypeStruct((rows, width), f32),
+        in_specs=[pl.BlockSpec(memory_space=pl.ANY)] * 5,
+        out_specs=pl.BlockSpec(memory_space=pltpu.VMEM),
+        scratch_shapes=scratch,
+        compiler_params=pltpu.CompilerParams(
+            collective_id=0, has_side_effects=True, vmem_limit_bytes=60 << 20),
+    )(right_side, solved_factor, solved_users, diag_inverse, coupling)
+
+
+def on_device(right_side, *others):
+    whole_tiles = right_side.shape[1] % LANES == 0 and lax.axis_size("col") % 2 == 0
+    return (by_kernel if whole_tiles else by_collectives)(right_side, *others)
+
+
 def solution(mesh):
     placed = (P("grp", "col"), P("grp", "col"), P("col", None), P("grp", None), P("grp", None))
     return jax.shard_map(

time: 240 us -> 86.4 us (0.36); the launches traced: 237 us -> 86.3 us
  waiting for transfers between devices: 185 us -> 0 us
  Pallas kernels: 0 us -> 84.4 us
  matrix products: 32.3 us -> 0 us
  between operations: 13.2 us -> 0.01 us
  local copies, waits for them, and re-layouts: 5.04 us -> 1.87 us
    psum x3 -> x0, waiting for transfers between devices: 135 us -> none  [broadcast(): return lax.psum(block, axis)]
    pallas_call x0 -> x1, Pallas kernels: none -> 84.4 us  [by_kernel(): pl.pallas_call(functools.partial(kernel, groups, chips, pieces), out_shap...]
    reduce_scatter x1 -> x0, waiting for transfers between devices: 49.3 us -> none  [on_device(): shares = lax.psum_scatter(partials, 'col', scatter_dimension=1, tiled=True)]
    dot_general x8 -> x0, matrix products: 32.3 us -> none  [the longest x7 18.6 us: apply_plain(): jnp.dot(matrix, vector, precision=highest, preferred_element_type=jnp.flo...]
  transfers between devices with their start and end apart: 4 -> 0, of which waited for: 4 -> 0; matrix products, arithmetic and copies ran while one was open for 0% -> 0% of each run, Pallas kernels for 0% -> 0%
where the time goes in v1:
time: 86.4 us; the launch traced here: 86.3 us
  Pallas kernels  84.4 us (98%)
  local copies, waits for them, and re-layouts  1.87 us (2%)
    pallas_call x1, Pallas kernels, by_kernel(): pl.pallas_call(functools.partial(kernel, groups, chips, pieces), out_shap...  84.4 us
    unnamed x1, local copies, waits for them, and re-layouts  1.87 us

profile of v1, /device:TPU:7, one launch (start us, length us, event | category | flops | bytes accessed | tf_op | source)
XLA Modules:
  0.0 86.3 jit_solution(15623097514674441721)
XLA Ops:
  0.0 84.4 %shard_map.55 = f32[512,256]{1,0:T(8,128)} custom-call(f32[512,256]{1,0:T(8,128)} %rhs_hbm.1, f32[512,768]{1,0:T(8,128)} %factor_hbm.1, f32[768,2048]{1,0:T(8,128)} %users_hbm.1, f32[512,512]{1,0:T(8,128)} %diag_hbm.1, f32[512,1536]{1,0:T(8,128)} %coupling_hbm.1), custom_call_target="tpu_custom_call" | custom-call | tf_op jit(solution)/shard_map/pallas_call | solution.py:346
  84.4 1.9 %copy.7 = f32[512,256]{1,0:T(8,128)} copy(f32[512,256]{1,0:T(8,128)} %shard_map.55) | data formatting | bytes 1048576

commit v2 on v1

--- a/solution.py
+++ b/solution.py
@@ -118,9 +118,6 @@
     def _(b):
         users_load(b).start()
 
-    for copy in later:
-        copy.start()
-
     barrier = pltpu.get_barrier_semaphore()
     pl.semaphore_signal(barrier, inc=1, device_id=partner, device_id_type=MESH)
     for step in range(1, groups):
@@ -197,14 +194,14 @@
             send_first(block_of(b), q)
 
     for copy in later:
-        copy.wait()
-    diag3[...] = left_form(diag[...])
-    for h in range(groups - 1):
+        copy.start()
+
+    def effect(h):
         @pl.loop(0, rows // (2 * LANES))
         def _(n):
             columns = pl.multiple_of(n * 2 * LANES, 2 * LANES)
-            product = dot(
-                diag3[...], right_form(coupling[:, pl.ds(h * rows + columns, 2 * LANES)]))
+            source = pl.multiple_of(h * rows + columns, 2 * LANES)
+            product = dot(diag3[...], right_form(coupling[:, pl.ds(source, 2 * LANES)]))
             high, low = halves(product)
             effect3[h, :, pl.ds(columns, 2 * LANES)] = high
             effect3[h, :, pl.ds(rows + columns, 2 * LANES)] = high
@@ -220,21 +217,33 @@
     def reduce_piece(p):
         q = p // 2
         side = p % 2
+
+        def relay_up():
+            for s in range(chips - 1):
+                i = side * chips + chips - 1 - s
+
+                @pl.when(jnp.logical_and(z > 0, chips - 1 - s > z))
+                def _():
+                    up(i, q).wait_recv()
+                    own[i, q] = own[i, q] + from_low[i, q]
+                    up(i, q).start()
+
+        @pl.when(2 * z < chips)
+        def _():
+            relay_up()
+
         for s in range(chips - 1):
-            right = side * chips + chips - 1 - s
-            left = side * chips + s
-
-            @pl.when(jnp.logical_and(z > 0, chips - 1 - s > z))
-            def _():
-                up(right, q).wait_recv()
-                own[right, q] = own[right, q] + from_low[right, q]
-                up(right, q).start()
+            i = side * chips + s
 
             @pl.when(jnp.logical_and(z < chips - 1, s < z))
             def _():
-                down(left, q).wait_recv()
-                own[left, q] = own[left, q] + from_high[left, q]
-                down(left, q).start()
+                down(i, q).wait_recv()
+                own[i, q] = own[i, q] + from_high[i, q]
+                down(i, q).start()
+
+        @pl.when(2 * z >= chips)
+        def _():
+            relay_up()
 
         mine = side * chips + z
 
@@ -286,11 +295,21 @@
         def _():
             reduce_piece(t)
 
+        @pl.when(t == 0)
+        def _():
+            for copy in later:
+                copy.wait()
+            diag3[...] = left_form(diag[...])
+
         p = t - g
 
         @pl.when(jnp.logical_and(jnp.logical_and(p >= 0, p < count), (p + 2 * groups) % 2 == e))
         def _():
             solve_piece(p // 2)
+
+        @pl.when(jnp.logical_and(t < groups - 1, t < g))
+        def _():
+            effect(t)
 
     @pl.loop(0, 2 * chips)
     def _(i):

time: 86.4 us -> 68 us (0.79)
  Pallas kernels: 84.4 us -> 65.9 us
    pallas_call x1, Pallas kernels: 84.4 us -> 65.9 us  [by_kernel(): pl.pallas_call(functools.partial(kernel, groups, chips, pieces), out_shap...]
where the time goes in v2:
time: 68 us; the launch traced here: 67.8 us
  Pallas kernels  65.9 us (97%)
  local copies, waits for them, and re-layouts  1.87 us (3%)
    pallas_call x1, Pallas kernels, by_kernel(): pl.pallas_call(functools.partial(kernel, groups, chips, pieces), out_shap...  65.9 us
    unnamed x1, local copies, waits for them, and re-layouts  1.87 us

profile of v2, /device:TPU:7, one launch (start us, length us, event | category | flops | bytes accessed | tf_op | source)
XLA Modules:
  0.0 67.8 jit_solution(4694440732354258489)
XLA Ops:
  0.0 65.9 %shard_map.55 = f32[512,256]{1,0:T(8,128)} custom-call(f32[512,256]{1,0:T(8,128)} %rhs_hbm.1, f32[512,768]{1,0:T(8,128)} %factor_hbm.1, f32[768,2048]{1,0:T(8,128)} %users_hbm.1, f32[512,512]{1,0:T(8,128)} %diag_hbm.1, f32[512,1536]{1,0:T(8,128)} %coupling_hbm.1), custom_call_target="tpu_custom_call" | custom-call | tf_op jit(solution)/shard_map/pallas_call | solution.py:365
  65.9 1.9 %copy.7 = f32[512,256]{1,0:T(8,128)} copy(f32[512,256]{1,0:T(8,128)} %shard_map.55) | data formatting | bytes 1048576

commit v3 on v2

--- a/solution.py
+++ b/solution.py
@@ -68,13 +68,30 @@
     return jnp.dot(a, b, preferred_element_type=jnp.float32)
 
 
+def swap(x):
+    return pltpu.roll(x, LANES // 2, 1)
+
+
+def first_lanes(shape):
+    return lax.broadcasted_iota(jnp.int32, shape, 1) < LANES // 2
+
+
+def pack(x):
+    upper, lower = x[: x.shape[0] // 2], x[x.shape[0] // 2 :]
+    return jnp.where(first_lanes(upper.shape), upper, swap(lower))
+
+
+def unpack(x):
+    return jnp.concatenate([x, swap(x)], axis=0)
+
+
 def kernel(
     groups, chips, pieces,
     rhs_hbm, factor_hbm, users_hbm, diag_hbm, coupling_hbm,
     out_ref,
     rhs, factor, users, diag, coupling,
     factor3, diag3, effect3,
-    own, give, take, from_low, from_high, total, spare, solved, arrived,
+    own, give, take, from_low, from_high, total, spare, work, solved, arrived,
     load_sem, users_sem, give_sem, take_sem, hop_sem, low_sem, high_sem,
     spare_sem, total_sem, solved_sem, arrived_sem,
 ):
@@ -132,12 +149,12 @@
     def _():
         pl.semaphore_signal(barrier, inc=1, device_id=above, device_id_type=MESH)
 
-    pl.semaphore_wait(
-        barrier, groups + jnp.where(z > 0, 1, 0) + jnp.where(z < chips - 1, 1, 0))
-
     for copy in loads:
         copy.wait()
     factor3[...] = left_form(factor[...])
+
+    pl.semaphore_wait(
+        barrier, groups + jnp.where(z > 0, 1, 0) + jnp.where(z < chips - 1, 1, 0))
 
     def give_copy(i):
         return pltpu.make_async_remote_copy(
@@ -266,26 +283,49 @@
             spare[q] = own[mine, q]
             total_copy(side, q).start()
 
-    def solved_copy(source, target, q):
+    def solved_copy(source, target, q, a):
         return pltpu.make_async_remote_copy(
-            src_ref=solved.at[q], dst_ref=arrived.at[source, q],
-            send_sem=solved_sem.at[target, q], recv_sem=arrived_sem.at[source, q],
+            src_ref=solved.at[q, a], dst_ref=arrived.at[source, q, a],
+            send_sem=solved_sem.at[target, q, a], recv_sem=arrived_sem.at[source, q, a],
             device_id=(target, c), device_id_type=MESH)
+
+    last = jnp.maximum(g - 1, 0)
 
     def solve_piece(q):
         columns = pl.ds(pl.multiple_of(q * LANES, LANES), LANES)
         total_copy(e, q).wait_recv()
-        solved[q] = dot(diag3[...], right_form(rhs[:, columns] - total[q]))
-        for h in range(groups - 1):
-            @pl.when(h < g)
-            def _():
-                solved_copy(h, 0, q).wait_recv()
-                solved[q] = solved[q] - dot(effect3[h], right_form(arrived[h, q]))
-        for target in range(1, groups):
-            @pl.when(target > g)
-            def _():
-                solved_copy(g, target, q).start()
-        out_ref[:, columns] = solved[q]
+        work[...] = dot(diag3[...], right_form(rhs[:, columns] - total[q]))
+        for h in range(groups - 2):
+            @pl.when(h < g - 1)
+            def _():
+                solved_copy(h, 0, q, 0).wait_recv()
+                solved_copy(h, 0, q, 1).wait_recv()
+                first = unpack(arrived[h, q, 0])
+                both = jnp.where(
+                    first_lanes(first.shape), first, swap(unpack(arrived[h, q, 1])))
+                work[...] = work[...] - dot(effect3[h], right_form(both))
+        for a in range(2):
+            @pl.when(g > 0)
+            def _():
+                solved_copy(last, 0, q, a).wait_recv()
+                product = dot(effect3[last], right_form(unpack(arrived[last, q, a])))
+                if a == 0:
+                    mine = first_lanes(product.shape)
+                else:
+                    product = swap(product)
+                    mine = jnp.logical_not(first_lanes(product.shape))
+                work[...] = jnp.where(mine, work[...] - product, work[...])
+
+            @pl.when(g < groups - 1)
+            def _():
+                solved[q, a] = pack(work[...] if a == 0 else swap(work[...]))
+                solved_copy(g, g + 1, q, a).start()
+        for target in range(2, groups):
+            @pl.when(target > g + 1)
+            def _():
+                for a in range(2):
+                    solved_copy(g, target, q, a).start()
+        out_ref[:, columns] = work[...]
 
     count = 2 * pieces
 
@@ -326,7 +366,8 @@
         for target in range(1, groups):
             @pl.when(target > g)
             def _():
-                solved_copy(g, target, q).wait_send()
+                for a in range(2):
+                    solved_copy(g, target, q, a).wait_send()
 
 
 def by_kernel(right_side, solved_factor, solved_users, diag_inverse, coupling):
@@ -356,11 +397,12 @@
         pltpu.VMEM((blocks, pieces) + unit, f32),
         pltpu.VMEM((pieces, rows, LANES), f32),
         pltpu.VMEM((pieces,) + unit, f32),
-        pltpu.VMEM((pieces, rows, LANES), f32),
-        pltpu.VMEM((groups - 1, pieces, rows, LANES), f32),
+        pltpu.VMEM((rows, LANES), f32),
+        pltpu.VMEM((pieces, 2) + unit, f32),
+        pltpu.VMEM((groups - 1, pieces, 2) + unit, f32),
         dma((5,)), dma((blocks,)), dma((blocks,)), dma((blocks,)),
         dma((blocks, pieces)), dma((blocks, pieces)), dma((blocks, pieces)),
-        dma((pieces,)), dma((pieces,)), dma((groups, pieces)), dma((groups, pieces)),
+        dma((pieces,)), dma((pieces,)), dma((groups, pieces, 2)), dma((groups, pieces, 2)),
     ]
     return pl.pallas_call(
         functools.partial(kernel, groups, chips, pieces),

time: 68 us -> 66.9 us (0.984)
  Pallas kernels: 65.9 us -> 64.6 us
    pallas_call x1, Pallas kernels: 65.9 us -> 64.6 us  [by_kernel(): pl.pallas_call(functools.partial(kernel, groups, chips, pieces), out_shap...]
where the time goes in v3:
time: 66.9 us; the launch traced here: 66.4 us
  Pallas kernels  64.6 us (97%)
  local copies, waits for them, and re-layouts  1.87 us (3%)
    pallas_call x1, Pallas kernels, by_kernel(): pl.pallas_call(functools.partial(kernel, groups, chips, pieces), out_shap...  64.6 us
    unnamed x1, local copies, waits for them, and re-layouts  1.87 us

profile of v3, /device:TPU:7, one launch (start us, length us, event | category | flops | bytes accessed | tf_op | source)
XLA Modules:
  0.0 66.4 jit_solution(17494367147079705625)
XLA Ops:
  0.0 64.6 %shard_map.55 = f32[512,256]{1,0:T(8,128)} custom-call(f32[512,256]{1,0:T(8,128)} %rhs_hbm.1, f32[512,768]{1,0:T(8,128)} %factor_hbm.1, f32[768,2048]{1,0:T(8,128)} %users_hbm.1, f32[512,512]{1,0:T(8,128)} %diag_hbm.1, f32[512,1536]{1,0:T(8,128)} %coupling_hbm.1), custom_call_target="tpu_custom_call" | custom-call | tf_op jit(solution)/shard_map/pallas_call | solution.py:407
  64.6 1.9 %copy.7 = f32[512,256]{1,0:T(8,128)} copy(f32[512,256]{1,0:T(8,128)} %shard_map.55) | data formatting | bytes 1048576

commit v4 on v3

--- a/solution.py
+++ b/solution.py
@@ -406,12 +406,12 @@
     ]
     return pl.pallas_call(
         functools.partial(kernel, groups, chips, pieces),
-        out_shape=jax.ShapeDtypeStruct((rows, width), f32),
+        out_shape=pltpu.VMEM((rows, width), f32),
         in_specs=[pl.BlockSpec(memory_space=pl.ANY)] * 5,
         out_specs=pl.BlockSpec(memory_space=pltpu.VMEM),
         scratch_shapes=scratch,
         compiler_params=pltpu.CompilerParams(
-            collective_id=0, has_side_effects=True, vmem_limit_bytes=60 << 20),
+            collective_id=0, has_side_effects=True, vmem_limit_bytes=63 << 20),
     )(right_side, solved_factor, solved_users, diag_inverse, coupling)
 
 

time: 66.9 us -> 65 us (0.972)
  local copies, waits for them, and re-layouts: 1.87 us -> 0.8 us
  Pallas kernels: 64.6 us -> 63.8 us
    unnamed x1, local copies, waits for them, and re-layouts: 1.87 us -> 0.8 us
    pallas_call x1, Pallas kernels: 64.6 us -> 63.8 us  [by_kernel(): pl.pallas_call(functools.partial(kernel, groups, chips, pieces), out_shap...]
where the time goes in v4:
time: 65 us; the launch traced here: 64.6 us
  Pallas kernels  63.8 us (98%)
  local copies, waits for them, and re-layouts  0.8 us (1%)
    pallas_call x1, Pallas kernels, by_kernel(): pl.pallas_call(functools.partial(kernel, groups, chips, pieces), out_shap...  63.8 us

profile of v4, /device:TPU:7, one launch (start us, length us, event | category | flops | bytes accessed | tf_op | source)
XLA Modules:
  0.0 64.6 jit_solution(3092249627308022970)
XLA Ops:
  0.0 63.8 %shard_map.55 = f32[512,256]{1,0:T(8,128)S(1)} custom-call(f32[512,256]{1,0:T(8,128)} %rhs_hbm.1, f32[512,768]{1,0:T(8,128)} %factor_hbm.1, f32[768,2048]{1,0:T(8,128)} %users_hbm.1, f32[512,512]{1,0:T(8,128)} %diag_hbm.1, f32[512,1536]{1,0:T(8,128)} %coupling_hbm.1), custom_call_target="tpu_custom_call" | custom-call | tf_op jit(solution)/shard_map/pallas_call | solution.py:407
  63.8 0.8 %copy.7 = f32[512,256]{1,0:T(8,128)} copy(f32[512,256]{1,0:T(8,128)S(1)} %shard_map.55) | data formatting | bytes 1048576

commit v5 on v2

--- a/solution.py
+++ b/solution.py
@@ -68,13 +68,30 @@
     return jnp.dot(a, b, preferred_element_type=jnp.float32)
 
 
+def swap(x):
+    return pltpu.roll(x, LANES // 2, 1)
+
+
+def first_lanes(shape):
+    return lax.broadcasted_iota(jnp.int32, shape, 1) < LANES // 2
+
+
+def pack(x):
+    upper, lower = x[: x.shape[0] // 2], x[x.shape[0] // 2 :]
+    return jnp.where(first_lanes(upper.shape), upper, swap(lower))
+
+
+def unpack(x):
+    return jnp.concatenate([x, swap(x)], axis=0)
+
+
 def kernel(
     groups, chips, pieces,
     rhs_hbm, factor_hbm, users_hbm, diag_hbm, coupling_hbm,
     out_ref,
     rhs, factor, users, diag, coupling,
     factor3, diag3, effect3,
-    own, give, take, from_low, from_high, total, spare, solved, arrived,
+    own, give, take, from_low, from_high, total, spare, work, solved, arrived,
     load_sem, users_sem, give_sem, take_sem, hop_sem, low_sem, high_sem,
     spare_sem, total_sem, solved_sem, arrived_sem,
 ):
@@ -118,6 +135,7 @@
     def _(b):
         users_load(b).start()
 
+    out_ref[...] = jnp.zeros_like(out_ref)
     barrier = pltpu.get_barrier_semaphore()
     pl.semaphore_signal(barrier, inc=1, device_id=partner, device_id_type=MESH)
     for step in range(1, groups):
@@ -132,12 +150,12 @@
     def _():
         pl.semaphore_signal(barrier, inc=1, device_id=above, device_id_type=MESH)
 
-    pl.semaphore_wait(
-        barrier, groups + jnp.where(z > 0, 1, 0) + jnp.where(z < chips - 1, 1, 0))
-
     for copy in loads:
         copy.wait()
     factor3[...] = left_form(factor[...])
+
+    pl.semaphore_wait(
+        barrier, groups + jnp.where(z > 0, 1, 0) + jnp.where(z < chips - 1, 1, 0))
 
     def give_copy(i):
         return pltpu.make_async_remote_copy(
@@ -177,10 +195,13 @@
         users_load(b).wait()
         i = block_of(b)
         product = dot(factor3[...], right_form(users[b]))
-        for q in range(pieces):
-            columns = slice(q * LANES, (q + 1) * LANES)
-            own[i, q] = product[:half, columns]
-            give[i, q] = product[half:, columns]
+        for k in range(pieces // 2):
+            tile = product[:, k * LANES : (k + 1) * LANES]
+            turned = swap(tile)
+            own[i, 2 * k] = pack(tile[:half])
+            own[i, 2 * k + 1] = pack(turned[:half])
+            give[i, 2 * k] = pack(tile[half:])
+            give[i, 2 * k + 1] = pack(turned[half:])
         give_copy(i).start()
 
         @pl.when(b > 0)
@@ -208,30 +229,22 @@
             effect3[h, :, pl.ds(2 * rows + columns, 2 * LANES)] = low
 
     def total_copy(side, q):
-        start = pl.multiple_of(e * half, half)
         return pltpu.make_async_remote_copy(
-            src_ref=spare.at[q], dst_ref=total.at[q, pl.ds(start, half)],
+            src_ref=spare.at[q], dst_ref=total.at[q, e],
             send_sem=spare_sem.at[q], recv_sem=total_sem.at[q],
             device_id=partner, device_id_type=MESH)
 
-    def reduce_piece(p):
-        q = p // 2
-        side = p % 2
-
-        def relay_up():
-            for s in range(chips - 1):
-                i = side * chips + chips - 1 - s
-
-                @pl.when(jnp.logical_and(z > 0, chips - 1 - s > z))
-                def _():
-                    up(i, q).wait_recv()
-                    own[i, q] = own[i, q] + from_low[i, q]
-                    up(i, q).start()
-
-        @pl.when(2 * z < chips)
-        def _():
-            relay_up()
-
+    def relay_up(q, side):
+        for s in range(chips - 1):
+            i = side * chips + chips - 1 - s
+
+            @pl.when(jnp.logical_and(z > 0, chips - 1 - s > z))
+            def _():
+                up(i, q).wait_recv()
+                own[i, q] = own[i, q] + from_low[i, q]
+                up(i, q).start()
+
+    def relay_down(q, side):
         for s in range(chips - 1):
             i = side * chips + s
 
@@ -241,9 +254,28 @@
                 own[i, q] = own[i, q] + from_high[i, q]
                 down(i, q).start()
 
-        @pl.when(2 * z >= chips)
-        def _():
-            relay_up()
+    lower = 2 * z < chips
+
+    def relay_near(p):
+        @pl.when(lower)
+        def _():
+            relay_up(p // 2, p % 2)
+
+        @pl.when(jnp.logical_not(lower))
+        def _():
+            relay_down(p // 2, p % 2)
+
+    def finish_piece(p):
+        q = p // 2
+        side = p % 2
+
+        @pl.when(lower)
+        def _():
+            relay_down(q, side)
+
+        @pl.when(jnp.logical_not(lower))
+        def _():
+            relay_up(q, side)
 
         mine = side * chips + z
 
@@ -259,7 +291,7 @@
 
         @pl.when(side == e)
         def _():
-            total[q, pl.ds(pl.multiple_of(e * half, half), half)] = own[mine, q]
+            total[q, e] = own[mine, q]
 
         @pl.when(side != e)
         def _():
@@ -273,27 +305,44 @@
             device_id=(target, c), device_id_type=MESH)
 
     def solve_piece(q):
-        columns = pl.ds(pl.multiple_of(q * LANES, LANES), LANES)
+        columns = pl.ds(pl.multiple_of((q // 2) * LANES, LANES), LANES)
+        odd = q % 2 == 1
+        right = rhs[:, columns]
+        right = jnp.where(odd, swap(right), right)
         total_copy(e, q).wait_recv()
-        solved[q] = dot(diag3[...], right_form(rhs[:, columns] - total[q]))
+        reduced = right - jnp.concatenate([unpack(total[q, 0]), unpack(total[q, 1])], axis=0)
+        work[...] = dot(diag3[...], right_form(reduced))
         for h in range(groups - 1):
             @pl.when(h < g)
             def _():
                 solved_copy(h, 0, q).wait_recv()
-                solved[q] = solved[q] - dot(effect3[h], right_form(arrived[h, q]))
+                work[...] = work[...] - dot(effect3[h], right_form(unpack(arrived[h, q])))
+        result = work[...]
+
+        @pl.when(g < groups - 1)
+        def _():
+            solved[q] = pack(result)
         for target in range(1, groups):
             @pl.when(target > g)
             def _():
                 solved_copy(g, target, q).start()
-        out_ref[:, columns] = solved[q]
+        placed = jnp.where(odd, swap(result), result)
+        mine = first_lanes(placed.shape) != odd
+        out_ref[:, columns] = jnp.where(mine, placed, out_ref[:, columns])
 
     count = 2 * pieces
+
+    relay_near(0)
 
     @pl.loop(0, count + groups - 1)
     def _(t):
+        @pl.when(t + 1 < count)
+        def _():
+            relay_near(t + 1)
+
         @pl.when(t < count)
         def _():
-            reduce_piece(t)
+            finish_piece(t)
 
         @pl.when(t == 0)
         def _():
@@ -335,9 +384,9 @@
     rows, width = right_side.shape
     depth = solved_factor.shape[1]
     half = rows // 2
-    pieces = width // LANES
+    pieces = width // (LANES // 2)
     f32, bf16 = jnp.float32, jnp.bfloat16
-    unit = (half, LANES)
+    unit = (half // 2, LANES)
     blocks = 2 * chips
     dma = pltpu.SemaphoreType.DMA
     scratch = [
@@ -354,22 +403,23 @@
         pltpu.VMEM((blocks, pieces) + unit, f32),
         pltpu.VMEM((blocks, pieces) + unit, f32),
         pltpu.VMEM((blocks, pieces) + unit, f32),
-        pltpu.VMEM((pieces, rows, LANES), f32),
+        pltpu.VMEM((pieces, 2) + unit, f32),
         pltpu.VMEM((pieces,) + unit, f32),
-        pltpu.VMEM((pieces, rows, LANES), f32),
-        pltpu.VMEM((groups - 1, pieces, rows, LANES), f32),
+        pltpu.VMEM((rows, LANES), f32),
+        pltpu.VMEM((pieces, half, LANES), f32),
+        pltpu.VMEM((groups - 1, pieces, half, LANES), f32),
         dma((5,)), dma((blocks,)), dma((blocks,)), dma((blocks,)),
         dma((blocks, pieces)), dma((blocks, pieces)), dma((blocks, pieces)),
         dma((pieces,)), dma((pieces,)), dma((groups, pieces)), dma((groups, pieces)),
     ]
     return pl.pallas_call(
         functools.partial(kernel, groups, chips, pieces),
-        out_shape=jax.ShapeDtypeStruct((rows, width), f32),
+        out_shape=pltpu.VMEM((rows, width), f32),
         in_specs=[pl.BlockSpec(memory_space=pl.ANY)] * 5,
         out_specs=pl.BlockSpec(memory_space=pltpu.VMEM),
         scratch_shapes=scratch,
         compiler_params=pltpu.CompilerParams(
-            collective_id=0, has_side_effects=True, vmem_limit_bytes=60 << 20),
+            collective_id=0, has_side_effects=True, vmem_limit_bytes=63 << 20),
     )(right_side, solved_factor, solved_users, diag_inverse, coupling)
 
 

time: 68 us -> 62.9 us (0.925)
  Pallas kernels: 65.9 us -> 62 us
  local copies, waits for them, and re-layouts: 1.87 us -> 0.8 us
    pallas_call x1, Pallas kernels: 65.9 us -> 62 us  [by_kernel(): pl.pallas_call(functools.partial(kernel, groups, chips, pieces), out_shap...]
    unnamed x1, local copies, waits for them, and re-layouts: 1.87 us -> 0.8 us
where the time goes in v5:
time: 62.9 us; the launch traced here: 62.8 us
  Pallas kernels  62 us (99%)
  local copies, waits for them, and re-layouts  0.8 us (1%)
    pallas_call x1, Pallas kernels, by_kernel(): pl.pallas_call(functools.partial(kernel, groups, chips, pieces), out_shap...  62 us

profile of v5, /device:TPU:7, one launch (start us, length us, event | category | flops | bytes accessed | tf_op | source)
XLA Modules:
  0.0 62.8 jit_solution(12211939258049811117)
XLA Ops:
  0.0 62.0 %shard_map.55 = f32[512,256]{1,0:T(8,128)S(1)} custom-call(f32[512,256]{1,0:T(8,128)} %rhs_hbm.1, f32[512,768]{1,0:T(8,128)} %factor_hbm.1, f32[768,2048]{1,0:T(8,128)} %users_hbm.1, f32[512,512]{1,0:T(8,128)} %diag_hbm.1, f32[512,1536]{1,0:T(8,128)} %coupling_hbm.1), custom_call_target="tpu_custom_call" | custom-call | tf_op jit(solution)/shard_map/pallas_call | solution.py:415
  62.0 0.8 %copy.7 = f32[512,256]{1,0:T(8,128)} copy(f32[512,256]{1,0:T(8,128)S(1)} %shard_map.55) | data formatting | bytes 1048576

commit v6 on v5

--- a/solution.py
+++ b/solution.py
@@ -157,10 +157,10 @@
     pl.semaphore_wait(
         barrier, groups + jnp.where(z > 0, 1, 0) + jnp.where(z < chips - 1, 1, 0))
 
-    def give_copy(i):
+    def give_copy(i, q):
         return pltpu.make_async_remote_copy(
-            src_ref=give.at[i], dst_ref=take.at[i], send_sem=give_sem.at[i],
-            recv_sem=take_sem.at[i], device_id=partner, device_id_type=MESH)
+            src_ref=give.at[i, q], dst_ref=take.at[i, q], send_sem=give_sem.at[i, q],
+            recv_sem=take_sem.at[i, q], device_id=partner, device_id_type=MESH)
 
     def up(i, q):
         return pltpu.make_async_remote_copy(
@@ -186,9 +186,11 @@
 
     def merge(b):
         i = block_of(b)
-        give_copy(i).wait()
-        own[i] = own[i] + take[i]
-        send_first(i, 0)
+        for q in range(pieces):
+            give_copy(i, q).wait()
+            own[i, q] = own[i, q] + take[i, q]
+            if q == 0:
+                send_first(i, 0)
 
     @pl.loop(0, 2 * chips)
     def _(b):
@@ -202,7 +204,8 @@
             own[i, 2 * k + 1] = pack(turned[:half])
             give[i, 2 * k] = pack(tile[half:])
             give[i, 2 * k + 1] = pack(turned[half:])
-        give_copy(i).start()
+        for q in range(pieces):
+            give_copy(i, q).start()
 
         @pl.when(b > 0)
         def _():
@@ -408,7 +411,7 @@
         pltpu.VMEM((rows, LANES), f32),
         pltpu.VMEM((pieces, half, LANES), f32),
         pltpu.VMEM((groups - 1, pieces, half, LANES), f32),
-        dma((5,)), dma((blocks,)), dma((blocks,)), dma((blocks,)),
+        dma((5,)), dma((blocks,)), dma((blocks, pieces)), dma((blocks, pieces)),
         dma((blocks, pieces)), dma((blocks, pieces)), dma((blocks, pieces)),
         dma((pieces,)), dma((pieces,)), dma((groups, pieces)), dma((groups, pieces)),
     ]

time: 62.9 us -> 62.6 us (level)
  no operation moved by 1% of the time
where the time goes in v6:
time: 62.6 us; the launch traced here: 62.5 us
  Pallas kernels  61.7 us (99%)
  local copies, waits for them, and re-layouts  0.8 us (1%)
    pallas_call x1, Pallas kernels, by_kernel(): pl.pallas_call(functools.partial(kernel, groups, chips, pieces), out_shap...  61.7 us

profile of v6, /device:TPU:7, one launch (start us, length us, event | category | flops | bytes accessed | tf_op | source)
XLA Modules:
  0.0 62.5 jit_solution(6125405132821020289)
XLA Ops:
  0.0 61.7 %shard_map.55 = f32[512,256]{1,0:T(8,128)S(1)} custom-call(f32[512,256]{1,0:T(8,128)} %rhs_hbm.1, f32[512,768]{1,0:T(8,128)} %factor_hbm.1, f32[768,2048]{1,0:T(8,128)} %users_hbm.1, f32[512,512]{1,0:T(8,128)} %diag_hbm.1, f32[512,1536]{1,0:T(8,128)} %coupling_hbm.1), custom_call_target="tpu_custom_call" | custom-call | tf_op jit(solution)/shard_map/pallas_call | solution.py:418
  61.7 0.8 %copy.7 = f32[512,256]{1,0:T(8,128)} copy(f32[512,256]{1,0:T(8,128)S(1)} %shard_map.55) | data formatting | bytes 1048576
